TPU v7x, 256 devices: a whole 4x4x8 slice. The times are simulated.
256 devices in a mesh: train: 16 (over y_lo, z), test: 16 (over x, y_hi, core).
Axes of the slice: x: 4, y: 4 (y_hi: 2, y_lo: 2; y = y_hi * 2 + y_lo), z: 8, core: 2. Of those that a mesh axis runs over, the one named last changes fastest.
Arguments:
- query_out: bfloat16 [4096, 3584], P('train', 'test'), may hold values from -16 to 16, as said below
- query_in: bfloat16 [4096, 3584], P('train', 'test'), may hold values from -6 to 6
- passage_out: bfloat16 [4096, 3584], P('train', 'test'), may hold values from -16 to 16, as said below
- passage_in_sum: bfloat16 [4096, 3584], P('train', 'test'), may hold values from -192 to 192
- passage_len: int32 [4096], P('train'), may hold values from 16 to 512
- positive: int32 [4096], P('train'), may hold values from 0 to 4095
- proj_in: bfloat16 [3584, 64], P('test'), may hold values from -0.09375 to 0.09375
- proj_out: bfloat16 [3584, 64], P('test'), may hold values from -0.09375 to 0.09375
- test_grads: bfloat16 [16384, 4096], P(('test', 'train')), may hold values from -6 to 6
Outputs:
- scores: float32 [4096, 16384], P('train', 'test')
Inputs may be any that keep to these rules, and one draw needn't show every extreme that they name: `query_out`: entries stay within the range. `passage_out`: entries stay within the range.
All inputs are finite; a program needn't handle non-finite values.
Results may differ from a plain program's by a relative error of at most 0.0034.
Values may be sent and summed in bfloat16 or wider, within the bound.
A program may use at most 64 MiB of HBM per device.

v0:
```python
import math
import jax
import jax.numpy as jnp
from jax import lax
from jax.sharding import PartitionSpec as P

D = 3584


def copy_for_each(value, axis):
    copies = jnp.broadcast_to(value, (lax.axis_size(axis), *value.shape))
    return lax.all_to_all(copies, axis, split_axis=0, concat_axis=0, tiled=True)


def laid_out(blocks, dim):
    dims = list(blocks.shape[1:])
    dims[dim] *= blocks.shape[0]
    return jnp.moveaxis(blocks, 0, dim).reshape(dims)


def gathered_copies(value, axis, dim):
    blocks = copy_for_each(value, axis)
    return laid_out(blocks, dim)


def taken_together(value, axis):
    return copy_for_each(value, axis).max(axis=0)


def over_copies(value, axis):
    everything = copy_for_each(value, axis)
    return jnp.sum(everything, axis=0)


def split_up(value, dim, count):
    dims = value.shape
    blocks = value.reshape(*dims[:dim], count, dims[dim] // count, *dims[dim + 1 :])
    return jnp.moveaxis(blocks, dim, 0)


def summed_on_arrival(value, axis, dim):
    count = lax.axis_size(axis)
    blocks = lax.all_to_all(split_up(value, dim, count), axis, 0, 0, tiled=True)
    return jnp.sum(blocks, axis=0)


def in_one(arrays, axis):
    ends = [0]
    for a in arrays:
        ends.append(ends[-1] + a.size)
    so_far = lax.psum(jnp.concatenate([a.ravel() for a in arrays]), axis)
    return tuple((so_far[b:e].reshape(a.shape) for a, b, e in zip(arrays, ends, ends[1:])))


def local(
    query_out,
    query_in,
    passage_out,
    passage_in_sum,
    passage_len,
    positive,
    proj_in,
    proj_out,
    test_grads,
):
    rank_size = proj_in.shape[1]
    logit_scale = 1.0 / math.sqrt(D)
    whole_pass = gathered_copies(passage_out, "train", 0)
    pass_block = lax.all_to_all(whole_pass, "test", split_axis=0, concat_axis=1, tiled=True)
    query_full = lax.all_gather(query_out, "test", axis=1, tiled=True)
    proj_full = gathered_copies(proj_out, "test", 0).astype(jnp.float32)
    block_logits = (
        lax.dot_general(
            query_full, pass_block, (((1,), (1,)), ((), ())), preferred_element_type=jnp.float32
        )
        * logit_scale
    )
    block_cols = block_logits.shape[1]
    block_top = taken_together(jnp.max(block_logits, axis=1), "test")
    block_exp = jnp.exp(block_logits - block_top[:, None])
    block_sum = over_copies(jnp.sum(block_exp, axis=1), "test")
    first_col = lax.axis_index("test") * block_cols
    col_index = lax.broadcasted_iota(jnp.int32, block_logits.shape, 1) + first_col
    block_hit = (col_index == positive[:, None]).astype(jnp.float32)
    block_grad = (block_exp / block_sum[:, None] - block_hit).astype(jnp.bfloat16)
    query_partial = (
        jnp.dot(block_grad, pass_block, preferred_element_type=jnp.float32) * logit_scale
    )
    out_query = jnp.dot(query_partial, proj_full, precision=lax.Precision.HIGHEST)
    pass_partial = (
        lax.dot_general(
            block_grad, query_full, (((0,), (0,)), ((), ())), preferred_element_type=jnp.float32
        )
        * logit_scale
    )
    pass_small = jnp.dot(pass_partial, proj_full, precision=lax.Precision.HIGHEST)
    padded = jnp.zeros((whole_pass.shape[0], rank_size), jnp.float32)
    padded = lax.dynamic_update_slice_in_dim(padded, pass_small, first_col, 0)
    out_pass = summed_on_arrival(padded, "train", 0)
    act_query = jnp.dot(query_in, proj_in, preferred_element_type=jnp.float32)
    act_pass = jnp.dot(passage_in_sum, proj_in, preferred_element_type=jnp.float32)
    act_query, act_pass, out_query, out_pass = in_one(
        (act_query, act_pass, out_query, out_pass), "test"
    )
    act_pass = act_pass / passage_len[:, None].astype(jnp.float32)
    stacked = jnp.stack((act_query, act_pass, out_query, out_pass), axis=1)
    row_count = stacked.shape[0]
    outer = (
        stacked[:, 0, :, None] * stacked[:, 2, None, :]
        + stacked[:, 1, :, None] * stacked[:, 3, None, :]
    )
    train_grads = outer.reshape(row_count, rank_size * rank_size).astype(jnp.bfloat16)
    return lax.dot_general(
        train_grads,
        lax.all_gather(test_grads, "train", axis=0, tiled=True),
        (((1,), (1,)), ((), ())),
        preferred_element_type=jnp.float32,
    )


def solution(mesh):
    return jax.shard_map(
        local,
        mesh=mesh,
        in_specs=(
            P("train", "test"),
            P("train", "test"),
            P("train", "test"),
            P("train", "test"),
            P("train"),
            P("train"),
            P("test", None),
            P("test", None),
            P(("test", "train"), None),
        ),
        out_specs=P("train", "test"),
        check_vma=False,
    )
```

profile of v0, /device:TPU:1, one launch (start us, length us, event | category | flops | bytes accessed | tf_op | source)
XLA Modules:
  0.0 403.7 jit_solution(1863392339717188709)
XLA Ops:
  7.4 2.4 broadcast_in_dim.19
  9.7 10.2 %all-to-all-start = ((bf16[16,256,224]{1,2,0:T(8,128)(2,1)}), bf16[16,256,224]{1,2,0:T(8,128)(2,1)}, u32[]{:S(2)}, u32[]{:S(2)}) async-start(bf16[16,256,224]{1,2,0:T(8,128)(2,1)} %broadcast_in_dim.19), calls=%async_computation | async-start | bytes 3670016 | tf_op jit(solution)/shard_map/all_to_all | solution.py:12
  20.0 0.7 all-gather.3.cloned.1.call-update
  20.7 41.4 %all-to-all-done = bf16[16,256,224]{1,2,0:T(8,128)(2,1)} async-done(((bf16[16,256,224]{1,2,0:T(8,128)(2,1)}), bf16[16,256,224]{1,2,0:T(8,128)(2,1)}, u32[]{:S(2)}, u32[]{:S(2)}) %all-to-all-start) | async-done | bytes 1835040 | tf_op jit(solution)/shard_map/all_to_all | solution.py:12
  62.0 9.3 %all-to-all-start.1 = ((bf16[16,256,224]{1,2,0:T(8,128)(2,1)}), bf16[16,256,224]{1,2,0:T(8,128)(2,1)S(1)}, u32[]{:S(2)}, u32[]{:S(2)}) async-start(bf16[16,256,224]{1,2,0:T(8,128)(2,1)} %all-to-all-done), calls=%async_computation.1 | async-start | bytes 3670016 | tf_op jit(solution)/shard_map/all_to_all | solution.py:69
  71.3 7.7 %all-gather.3.cloned.1.call-done = bf16[256,3584]{0,1:T(8,128)(2,1)} async-done(((bf16[256,224]{0,1:T(8,128)(2,1)}), bf16[256,3584]{0,1:T(8,128)(2,1)}) %all-gather.3.cloned.1.call-update) | async-done | bytes 1835024 | tf_op jit(solution)/shard_map/all_gather | solution.py:70
  79.0 17.8 %all-to-all-done.1 = bf16[16,256,224]{1,2,0:T(8,128)(2,1)S(1)} async-done(((bf16[16,256,224]{1,2,0:T(8,128)(2,1)}), bf16[16,256,224]{1,2,0:T(8,128)(2,1)S(1)}, u32[]{:S(2)}, u32[]{:S(2)}) %all-to-all-start.1) | async-done | bytes 1835040 | tf_op jit(solution)/shard_map/all_to_all | solution.py:69
  96.9 2.4 fusion.2
  99.2 13.2 %all_to_all.43 = f32[16,1,256]{2,1,0:T(1,128)S(1)} all-to-all(f32[16,1,256]{2,1,0:T(1,128)S(1)} %broadcast_in_dim.20), channel_id=1, replica_groups=mesh['train'=16,'test'=16] {'test'}, dimensions={0} | all-to-all | bytes 32768 | tf_op jit(solution)/shard_map/all_to_all | solution.py:12
  112.4 0.8 broadcast_in_dim.22
  113.3 3.8 all-to-all-start.4
  117.2 11.1 %all-to-all-done.4 = bf16[16,224,64]{1,2,0:T(8,128)(2,1)S(1)} async-done(((bf16[16,224,64]{1,2,0:T(8,128)(2,1)}), bf16[16,224,64]{1,2,0:T(8,128)(2,1)S(1)}, u32[]{:S(2)}, u32[]{:S(2)}) %all-to-all-start.4) | async-done | bytes 458784 | tf_op jit(solution)/shard_map/all_to_all | solution.py:12
  128.9 4.5 %all-to-all-start.3 = ((f32[16,1,256]{2,1,0:T(1,128)}), f32[16,1,256]{2,1,0:T(1,128)S(1)}, u32[]{:S(2)}, u32[]{:S(2)}) async-start(f32[16,1,256]{2,1,0:T(1,128)} %broadcast_in_dim.21), calls=%async_computation.3 | async-start | bytes 32768 | tf_op jit(solution)/shard_map/all_to_all | solution.py:12
  133.4 1.1 copy.55
  134.5 1.9 reshape.84
  136.4 4.4 %all-to-all-done.3 = f32[16,1,256]{2,1,0:T(1,128)S(1)} async-done(((f32[16,1,256]{2,1,0:T(1,128)}), f32[16,1,256]{2,1,0:T(1,128)S(1)}, u32[]{:S(2)}, u32[]{:S(2)}) %all-to-all-start.3) | async-done | bytes 16416 | tf_op jit(solution)/shard_map/all_to_all | solution.py:12
  140.8 2.2 convolution_multiply_fusion
  143.1 2.0 convolution_dynamic-update-slice_fusion
  145.1 1.1 copy.72
  146.2 4.8 %all-to-all-start.5 = ((f32[16,256,64]{1,2,0:T(8,128)}), f32[16,256,64]{1,2,0:T(8,128)S(1)}, u32[]{:S(2)}, u32[]{:S(2)}) async-start(f32[16,256,64]{1,2,0:T(8,128)} %bitcast.26), calls=%async_computation.5 | async-start | bytes 2097152 | tf_op jit(solution)/shard_map/all_to_all | solution.py:43
  151.1 0.9 fusion.3
  152.0 1.0 reshape.82
  153.0 1.8 fusion.4
  154.7 1.6 reshape.83
  156.3 1.8 convolution_multiply_fusion.1
  158.1 1.8 fusion.5
  160.0 16.6 %all-to-all-done.5 = f32[16,256,64]{1,2,0:T(8,128)S(1)} async-done(((f32[16,256,64]{1,2,0:T(8,128)}), f32[16,256,64]{1,2,0:T(8,128)S(1)}, u32[]{:S(2)}, u32[]{:S(2)}) %all-to-all-start.5) | async-done | bytes 1048608 | tf_op jit(solution)/shard_map/all_to_all | solution.py:43
  176.9 0.7 pad_maximum_fusion
  178.2 208.8 %all-reduce.2.cloned.1.call-done = f32[65536]{0:T(1024)} async-done(((f32[65536]{0:T(1024)}), f32[65536]{0:T(1024)}) %all-reduce.2.cloned.1.call-update) | async-done | bytes 262160 | tf_op jit(solution)/shard_map/psum | solution.py:51
  387.0 1.0 fusion.1
  388.7 0.7 add_convert_fusion
  389.5 6.7 %fusion.6 = f32[256,1024]{1,0:T(8,128)} fusion(bf16[256,4096]{0,1:T(8,128)(2,1)S(1)} %bitcast.28, bf16[1024,4096]{1,0:T(8,128)(2,1)} %all-gather.5.cloned.1.call-done), kind=kOutput, calls=%fused_computation.17 | convolution fusion | flops 2147483648 | bytes 11534336 | tf_op jit(solution)/shard_map/dot_general | solution.py:113
  (47 shorter events, 2.6 us)
Async XLA Ops:
  7.4 143.7 %copy-start = (bf16[256,224]{0,1:T(8,128)(2,1)S(1)}, bf16[256,224]{0,1:T(8,128)(2,1)}, u32[]{:S(2)}) copy-start(bf16[256,224]{0,1:T(8,128)(2,1)} %param.10) | copy-start | bytes 344068
  9.7 52.3 %all-to-all-start = ((bf16[16,256,224]{1,2,0:T(8,128)(2,1)}), bf16[16,256,224]{1,2,0:T(8,128)(2,1)}, u32[]{:S(2)}, u32[]{:S(2)}) async-start(bf16[16,256,224]{1,2,0:T(8,128)(2,1)} %broadcast_in_dim.19), calls=%async_computation | async-start | bytes 3670016 | tf_op jit(solution)/shard_map/all_to_all | solution.py:12
  19.9 59.1 %all-gather.3.cloned.1.call-start = ((), (), s32[]{:S(2)}) async-start(), calls=%async_computation.6 | async-start | bytes 1949696 | tf_op jit(solution)/shard_map/all_gather | solution.py:70
  20.6 91.8 %copy-start.4 = (bf16[224,64]{0,1:T(8,128)(2,1)S(1)}, bf16[224,64]{0,1:T(8,128)(2,1)}, u32[]{:S(2)}) copy-start(bf16[224,64]{0,1:T(8,128)(2,1)} %param.16) | copy-start | bytes 86020
  62.0 34.8 %all-to-all-start.1 = ((bf16[16,256,224]{1,2,0:T(8,128)(2,1)}), bf16[16,256,224]{1,2,0:T(8,128)(2,1)S(1)}, u32[]{:S(2)}, u32[]{:S(2)}) async-start(bf16[16,256,224]{1,2,0:T(8,128)(2,1)} %all-to-all-done), calls=%async_computation.1 | async-start | bytes 3670016 | tf_op jit(solution)/shard_map/all_to_all | solution.py:69
  96.9 44.0 %copy-start.7 = (s32[256]{0:T(256)S(1)}, s32[256]{0:T(256)}, u32[]{:S(2)}) copy-start(s32[256]{0:T(256)} %param.14) | copy-start | bytes 3076
  99.2 43.8 %copy-start.1 = (f32[256,256]{0,1:T(8,128)}, f32[256,256]{0,1:T(8,128)S(1)}, u32[]{:S(2)}) copy-start(f32[256,256]{0,1:T(8,128)S(1)} %get-tuple-element.10) | copy-start | bytes 786436
  113.3 15.0 %all-to-all-start.4 = ((bf16[16,224,64]{1,2,0:T(8,128)(2,1)}), bf16[16,224,64]{1,2,0:T(8,128)(2,1)S(1)}, u32[]{:S(2)}, u32[]{:S(2)}) async-start(bf16[16,224,64]{1,2,0:T(8,128)(2,1)} %broadcast_in_dim.22), calls=%async_computation.4 | async-start | bytes 1048576 | tf_op jit(solution)/shard_map/all_to_all | solution.py:12
  117.1 26.0 %copy-start.5 = (f32[256]{0:T(256)}, f32[256]{0:T(256)S(1)}, u32[]{:S(2)}) copy-start(f32[256]{0:T(256)S(1)} %reduce_max.19) | copy-start | bytes 3076
  128.9 11.9 %all-to-all-start.3 = ((f32[16,1,256]{2,1,0:T(1,128)}), f32[16,1,256]{2,1,0:T(1,128)S(1)}, u32[]{:S(2)}, u32[]{:S(2)}) async-start(f32[16,1,256]{2,1,0:T(1,128)} %broadcast_in_dim.21), calls=%async_computation.3 | async-start | bytes 32768 | tf_op jit(solution)/shard_map/all_to_all | solution.py:12
  133.4 9.6 %copy-start.8 = (s32[256]{0:T(256)}, s32[256]{0:T(256)S(1)}, u32[]{:S(2)}) copy-start(s32[256]{0:T(256)S(1)} %iota_add_fusion) | copy-start | bytes 3076
  140.8 4.3 %copy-start.6 = (f32[256]{0:T(256)}, f32[256]{0:T(256)S(1)}, u32[]{:S(2)}) copy-start(f32[256]{0:T(256)S(1)} %reduce_sum.28) | copy-start | bytes 3076
  143.1 7.9 %copy-start.3 = (bf16[224,64]{0,1:T(8,128)(2,1)S(1)}, bf16[224,64]{0,1:T(8,128)(2,1)}, u32[]{:S(2)}) copy-start(bf16[224,64]{0,1:T(8,128)(2,1)} %param.15) | copy-start | bytes 86020
  146.2 30.4 %all-to-all-start.5 = ((f32[16,256,64]{1,2,0:T(8,128)}), f32[16,256,64]{1,2,0:T(8,128)S(1)}, u32[]{:S(2)}, u32[]{:S(2)}) async-start(f32[16,256,64]{1,2,0:T(8,128)} %bitcast.26), calls=%async_computation.5 | async-start | bytes 2097152 | tf_op jit(solution)/shard_map/all_to_all | solution.py:43
  151.0 235.9 %all-reduce.2.cloned.1.call-start = ((), (), s32[]{:S(2)}) async-start(), calls=%async_computation.7 | async-start | bytes 524288 | tf_op jit(solution)/shard_map/psum | solution.py:51
  158.1 18.7 %copy-start.2 = (f32[16384]{0:T(1024)S(1)}, f32[16384]{0:T(1024)}, u32[]{:S(2)}) copy-start(f32[16384]{0:T(1024)} %reshape.83) | copy-start | bytes 196612
  158.1 20.1 %copy-start.9 = (s32[256]{0:T(256)S(1)}, s32[256]{0:T(256)}, u32[]{:S(2)}) copy-start(s32[256]{0:T(256)} %param.13) | copy-start | bytes 3076
  177.6 211.9 %all-gather.5.cloned.1.call-start = ((), (), s32[]{:S(2)}) async-start(), calls=%async_computation.8 | async-start | bytes 8912896 | tf_op jit(solution)/shard_map/all_gather | solution.py:115
Sparse Core Ops, SparseCore 0:
  23.4 55.5 all-gather.2
  177.7 209.1 all-reduce.1
Sparse Core Ops, SparseCore 1:
  179.9 97.2 all-gather.4
where the time goes:
time: 404 us
  waiting for transfers between devices  309 us (76%)
  starting transfers between devices  32.9 us (8%)
  matrix products  19.4 us (5%)
  between operations  15.2 us (4%)
  blocking collectives  13.2 us (3%)
  local copies, waits for them, and re-layouts  12.5 us (3%)
    psum x1, waiting for transfers between devices, in_one(): so_far = lax.psum(jnp.concatenate([a.ravel() for a in arrays]), axis)  209 us
    all_to_all x3, waiting for transfers between devices, copy_for_each(): return lax.all_to_all(copies, axis, split_axis=0, concat_axis=0, tiled=True)  56.9 us
    all_to_all x3, starting transfers between devices, copy_for_each(): return lax.all_to_all(copies, axis, split_axis=0, concat_axis=0, tiled=True)  18.4 us
    all_to_all x1, waiting for transfers between devices, local(): lax.all_to_all(whole_pass, 'test', split_axis=0, concat_axis=1, tiled=True)  17.8 us
    all_to_all x1, waiting for transfers between devices, summed_on_arrival(): blocks = lax.all_to_all(split_up(value, dim, count), axis, 0, 0, tiled=True)  16.6 us
    all_to_all x1, blocking collectives, copy_for_each(): return lax.all_to_all(copies, axis, split_axis=0, concat_axis=0, tiled=True)  13.2 us
    all_to_all x1, starting transfers between devices, local(): lax.all_to_all(whole_pass, 'test', split_axis=0, concat_axis=1, tiled=True)  9.32 us
  transfers between devices with their start and end apart: 8, of which 7 were waited for; matrix products, arithmetic and copies ran while one was open for 4% of the time, Pallas kernels for 0%

commit v1 on v0

--- a/solution.py
+++ b/solution.py
@@ -48,7 +48,7 @@
     ends = [0]
     for a in arrays:
         ends.append(ends[-1] + a.size)
-    so_far = lax.psum(jnp.concatenate([a.ravel() for a in arrays]), axis)
+    so_far = jnp.sum(lax.all_gather(jnp.concatenate([a.ravel() for a in arrays]), axis), axis=0)
     return tuple((so_far[b:e].reshape(a.shape) for a, b, e in zip(arrays, ends, ends[1:])))
 
 

time: 404 us -> 350 us (0.87)
  waiting for transfers between devices: 309 us -> 250 us
    psum x1 -> x0, waiting for transfers between devices: 209 us -> none  [in_one(): so_far = lax.psum(jnp.concatenate([a.ravel() for a in arrays]), axis)]
    all_gather x1, waiting for transfers between devices: 0.03 us -> 92.7 us  [local(): lax.all_gather(test_grads, 'train', axis=0, tiled=True)]
    all_gather x0 -> x1, waiting for transfers between devices: none -> 57.2 us  [in_one(): lax.all_gather(jnp.concatenate([a.ravel() for a in arrays]), axis)]
  transfers between devices with their start and end apart: 8 -> 8, of which waited for: 7 -> 8; matrix products, arithmetic and copies ran while one was open for 4% -> 6% of each run, Pallas kernels for 0% -> 0%
where the time goes in v1:
time: 350 us; the launch traced here: 349 us
  waiting for transfers between devices  250 us (71%)
  starting transfers between devices  32.9 us (9%)
  matrix products  19.4 us (6%)
  local copies, waits for them, and re-layouts  15.4 us (4%)
  between operations  13.4 us (4%)
  blocking collectives  13.2 us (4%)
  other arithmetic  4.66 us (1%)
    all_gather x1, waiting for transfers between devices, local(): lax.all_gather(test_grads, 'train', axis=0, tiled=True)  92.7 us
    all_gather x1, waiting for transfers between devices, in_one(): lax.all_gather(jnp.concatenate([a.ravel() for a in arrays]), axis)  57.2 us
    all_to_all x3, waiting for transfers between devices, copy_for_each(): return lax.all_to_all(copies, axis, split_axis=0, concat_axis=0, tiled=True)  56.9 us
    all_to_all x3, starting transfers between devices, copy_for_each(): return lax.all_to_all(copies, axis, split_axis=0, concat_axis=0, tiled=True)  18.4 us
    all_to_all x1, waiting for transfers between devices, local(): lax.all_to_all(whole_pass, 'test', split_axis=0, concat_axis=1, tiled=True)  17.8 us
    all_to_all x1, waiting for transfers between devices, summed_on_arrival(): blocks = lax.all_to_all(split_up(value, dim, count), axis, 0, 0, tiled=True)  16.6 us
    all_to_all x1, blocking collectives, copy_for_each(): return lax.all_to_all(copies, axis, split_axis=0, concat_axis=0, tiled=True)  13.2 us
    all_to_all x1, starting transfers between devices, local(): lax.all_to_all(whole_pass, 'test', split_axis=0, concat_axis=1, tiled=True)  9.32 us
  transfers between devices with their start and end apart: 8, of which 8 were waited for; matrix products, arithmetic and copies ran while one was open for 6% of the time, Pallas kernels for 0%

profile of v1, /device:TPU:1, one launch (start us, length us, event | category | flops | bytes accessed | tf_op | source)
XLA Modules:
  0.0 349.0 jit_solution(6144359740920412831)
XLA Ops:
  6.5 2.4 broadcast_in_dim.19
  8.9 10.2 %all-to-all-start = ((bf16[16,256,224]{1,2,0:T(8,128)(2,1)}), bf16[16,256,224]{1,2,0:T(8,128)(2,1)}, u32[]{:S(2)}, u32[]{:S(2)}) async-start(bf16[16,256,224]{1,2,0:T(8,128)(2,1)} %broadcast_in_dim.19), calls=%async_computation | async-start | bytes 3670016 | tf_op jit(solution)/shard_map/all_to_all | solution.py:12
  19.8 41.4 %all-to-all-done = bf16[16,256,224]{1,2,0:T(8,128)(2,1)} async-done(((bf16[16,256,224]{1,2,0:T(8,128)(2,1)}), bf16[16,256,224]{1,2,0:T(8,128)(2,1)}, u32[]{:S(2)}, u32[]{:S(2)}) %all-to-all-start) | async-done | bytes 1835040 | tf_op jit(solution)/shard_map/all_to_all | solution.py:12
  61.2 9.3 %all-to-all-start.1 = ((bf16[16,256,224]{1,2,0:T(8,128)(2,1)}), bf16[16,256,224]{1,2,0:T(8,128)(2,1)S(1)}, u32[]{:S(2)}, u32[]{:S(2)}) async-start(bf16[16,256,224]{1,2,0:T(8,128)(2,1)} %all-to-all-done), calls=%async_computation.1 | async-start | bytes 3670016 | tf_op jit(solution)/shard_map/all_to_all | solution.py:69
  70.5 7.7 %all-gather.5.cloned.1.call-done = bf16[256,3584]{0,1:T(8,128)(2,1)} async-done(((bf16[256,224]{0,1:T(8,128)(2,1)}), bf16[256,3584]{0,1:T(8,128)(2,1)}) %all-gather.5.cloned.1.call-update) | async-done | bytes 1835024 | tf_op jit(solution)/shard_map/all_gather | solution.py:70
  78.2 17.8 %all-to-all-done.1 = bf16[16,256,224]{1,2,0:T(8,128)(2,1)S(1)} async-done(((bf16[16,256,224]{1,2,0:T(8,128)(2,1)}), bf16[16,256,224]{1,2,0:T(8,128)(2,1)S(1)}, u32[]{:S(2)}, u32[]{:S(2)}) %all-to-all-start.1) | async-done | bytes 1835040 | tf_op jit(solution)/shard_map/all_to_all | solution.py:69
  96.0 2.4 fusion.2
  98.4 13.2 %all_to_all.43 = f32[16,1,256]{2,1,0:T(1,128)S(1)} all-to-all(f32[16,1,256]{2,1,0:T(1,128)S(1)} %broadcast_in_dim.20), channel_id=1, replica_groups=mesh['train'=16,'test'=16] {'test'}, dimensions={0} | all-to-all | bytes 32768 | tf_op jit(solution)/shard_map/all_to_all | solution.py:12
  111.6 0.8 broadcast_in_dim.22
  112.5 3.8 %all-to-all-start.4 = ((bf16[16,224,64]{1,2,0:T(8,128)(2,1)}), bf16[16,224,64]{1,2,0:T(8,128)(2,1)S(1)}, u32[]{:S(2)}, u32[]{:S(2)}) async-start(bf16[16,224,64]{1,2,0:T(8,128)(2,1)} %broadcast_in_dim.22), calls=%async_computation.4 | async-start | bytes 1048576 | tf_op jit(solution)/shard_map/all_to_all | solution.py:12
  116.3 11.1 %all-to-all-done.4 = bf16[16,224,64]{1,2,0:T(8,128)(2,1)S(1)} async-done(((bf16[16,224,64]{1,2,0:T(8,128)(2,1)}), bf16[16,224,64]{1,2,0:T(8,128)(2,1)S(1)}, u32[]{:S(2)}, u32[]{:S(2)}) %all-to-all-start.4) | async-done | bytes 458784 | tf_op jit(solution)/shard_map/all_to_all | solution.py:12
  128.1 4.5 %all-to-all-start.3 = ((f32[16,1,256]{2,1,0:T(1,128)}), f32[16,1,256]{2,1,0:T(1,128)S(1)}, u32[]{:S(2)}, u32[]{:S(2)}) async-start(f32[16,1,256]{2,1,0:T(1,128)} %broadcast_in_dim.21), calls=%async_computation.3 | async-start | bytes 32768 | tf_op jit(solution)/shard_map/all_to_all | solution.py:12
  132.6 1.1 copy.55
  133.7 1.9 reshape.84
  135.6 4.4 %all-to-all-done.3 = f32[16,1,256]{2,1,0:T(1,128)S(1)} async-done(((f32[16,1,256]{2,1,0:T(1,128)}), f32[16,1,256]{2,1,0:T(1,128)S(1)}, u32[]{:S(2)}, u32[]{:S(2)}) %all-to-all-start.3) | async-done | bytes 16416 | tf_op jit(solution)/shard_map/all_to_all | solution.py:12
  140.0 2.2 convolution_multiply_fusion
  142.3 2.0 convolution_dynamic-update-slice_fusion
  144.3 1.1 copy.72
  145.4 4.8 %all-to-all-start.5 = ((f32[16,256,64]{1,2,0:T(8,128)}), f32[16,256,64]{1,2,0:T(8,128)S(1)}, u32[]{:S(2)}, u32[]{:S(2)}) async-start(f32[16,256,64]{1,2,0:T(8,128)} %bitcast.26), calls=%async_computation.5 | async-start | bytes 2097152 | tf_op jit(solution)/shard_map/all_to_all | solution.py:43
  150.3 0.9 fusion.3
  151.1 1.0 reshape.82
  152.1 1.8 fusion.4
  153.9 1.6 reshape.83
  155.5 1.8 convolution_multiply_fusion.1
  157.3 1.8 fusion.5
  159.2 16.6 %all-to-all-done.5 = f32[16,256,64]{1,2,0:T(8,128)S(1)} async-done(((f32[16,256,64]{1,2,0:T(8,128)}), f32[16,256,64]{1,2,0:T(8,128)S(1)}, u32[]{:S(2)}, u32[]{:S(2)}) %all-to-all-start.5) | async-done | bytes 1048608 | tf_op jit(solution)/shard_map/all_to_all | solution.py:43
  177.5 57.2 %all-gather.9.cloned.1.call-done = f32[1048576]{0:T(1024)} async-done(((f32[65536]{0:T(1024)}), f32[1048576]{0:T(1024)}) %all-gather.9.cloned.1.call-update) | async-done | bytes 4194320 | tf_op jit(solution)/shard_map/all_gather | solution.py:51
  234.7 3.9 %reshape.88 = f32[16,65536]{1,0:T(8,128)} reshape(f32[1048576]{0:T(1024)} %all-gather.9.cloned.1.call-done) | data formatting | bytes 8388608 | tf_op jit(solution)/shard_map/all_gather | solution.py:51
  238.6 2.9 reduce_sum.39
  242.4 0.7 add_convert_fusion
  243.1 92.7 %all-gather.7.cloned.1.call-done = bf16[1024,4096]{1,0:T(8,128)(2,1)} async-done(((bf16[64,4096]{1,0:T(8,128)(2,1)}), bf16[1024,4096]{1,0:T(8,128)(2,1)}) %all-gather.7.cloned.1.call-update) | async-done | bytes 8388624 | tf_op jit(solution)/shard_map/all_gather | solution.py:115
  335.8 6.7 %fusion.6 = f32[256,1024]{1,0:T(8,128)} fusion(bf16[256,4096]{0,1:T(8,128)(2,1)S(1)} %bitcast.28, bf16[1024,4096]{1,0:T(8,128)(2,1)} %all-gather.7.cloned.1.call-done), kind=kOutput, calls=%fused_computation.17 | convolution fusion | flops 2147483648 | bytes 11534336 | tf_op jit(solution)/shard_map/dot_general | solution.py:113
  (49 shorter events, 4.2 us)
Async XLA Ops:
  6.5 143.7 %copy-start = (bf16[256,224]{0,1:T(8,128)(2,1)S(1)}, bf16[256,224]{0,1:T(8,128)(2,1)}, u32[]{:S(2)}) copy-start(bf16[256,224]{0,1:T(8,128)(2,1)} %param.10) | copy-start | bytes 344068
  8.9 52.3 %all-to-all-start = ((bf16[16,256,224]{1,2,0:T(8,128)(2,1)}), bf16[16,256,224]{1,2,0:T(8,128)(2,1)}, u32[]{:S(2)}, u32[]{:S(2)}) async-start(bf16[16,256,224]{1,2,0:T(8,128)(2,1)} %broadcast_in_dim.19), calls=%async_computation | async-start | bytes 3670016 | tf_op jit(solution)/shard_map/all_to_all | solution.py:12
  19.1 59.1 %all-gather.5.cloned.1.call-start = ((), (), s32[]{:S(2)}) async-start(), calls=%async_computation.6 | async-start | bytes 1949696 | tf_op jit(solution)/shard_map/all_gather | solution.py:70
  19.8 91.8 %copy-start.4 = (bf16[224,64]{0,1:T(8,128)(2,1)S(1)}, bf16[224,64]{0,1:T(8,128)(2,1)}, u32[]{:S(2)}) copy-start(bf16[224,64]{0,1:T(8,128)(2,1)} %param.16) | copy-start | bytes 86020
  61.2 34.8 %all-to-all-start.1 = ((bf16[16,256,224]{1,2,0:T(8,128)(2,1)}), bf16[16,256,224]{1,2,0:T(8,128)(2,1)S(1)}, u32[]{:S(2)}, u32[]{:S(2)}) async-start(bf16[16,256,224]{1,2,0:T(8,128)(2,1)} %all-to-all-done), calls=%async_computation.1 | async-start | bytes 3670016 | tf_op jit(solution)/shard_map/all_to_all | solution.py:69
  96.0 44.0 %copy-start.7 = (s32[256]{0:T(256)S(1)}, s32[256]{0:T(256)}, u32[]{:S(2)}) copy-start(s32[256]{0:T(256)} %param.14) | copy-start | bytes 3076
  98.4 43.8 %copy-start.1 = (f32[256,256]{0,1:T(8,128)}, f32[256,256]{0,1:T(8,128)S(1)}, u32[]{:S(2)}) copy-start(f32[256,256]{0,1:T(8,128)S(1)} %get-tuple-element.10) | copy-start | bytes 786436
  112.5 15.0 %all-to-all-start.4 = ((bf16[16,224,64]{1,2,0:T(8,128)(2,1)}), bf16[16,224,64]{1,2,0:T(8,128)(2,1)S(1)}, u32[]{:S(2)}, u32[]{:S(2)}) async-start(bf16[16,224,64]{1,2,0:T(8,128)(2,1)} %broadcast_in_dim.22), calls=%async_computation.4 | async-start | bytes 1048576 | tf_op jit(solution)/shard_map/all_to_all | solution.py:12
  116.2 26.0 %copy-start.5 = (f32[256]{0:T(256)}, f32[256]{0:T(256)S(1)}, u32[]{:S(2)}) copy-start(f32[256]{0:T(256)S(1)} %reduce_max.19) | copy-start | bytes 3076
  128.1 11.9 %all-to-all-start.3 = ((f32[16,1,256]{2,1,0:T(1,128)}), f32[16,1,256]{2,1,0:T(1,128)S(1)}, u32[]{:S(2)}, u32[]{:S(2)}) async-start(f32[16,1,256]{2,1,0:T(1,128)} %broadcast_in_dim.21), calls=%async_computation.3 | async-start | bytes 32768 | tf_op jit(solution)/shard_map/all_to_all | solution.py:12
  132.6 9.6 %copy-start.8 = (s32[256]{0:T(256)}, s32[256]{0:T(256)S(1)}, u32[]{:S(2)}) copy-start(s32[256]{0:T(256)S(1)} %iota_add_fusion) | copy-start | bytes 3076
  140.0 4.3 %copy-start.6 = (f32[256]{0:T(256)}, f32[256]{0:T(256)S(1)}, u32[]{:S(2)}) copy-start(f32[256]{0:T(256)S(1)} %reduce_sum.37) | copy-start | bytes 3076
  142.3 7.9 %copy-start.3 = (bf16[224,64]{0,1:T(8,128)(2,1)S(1)}, bf16[224,64]{0,1:T(8,128)(2,1)}, u32[]{:S(2)}) copy-start(bf16[224,64]{0,1:T(8,128)(2,1)} %param.15) | copy-start | bytes 86020
  145.4 30.4 %all-to-all-start.5 = ((f32[16,256,64]{1,2,0:T(8,128)}), f32[16,256,64]{1,2,0:T(8,128)S(1)}, u32[]{:S(2)}, u32[]{:S(2)}) async-start(f32[16,256,64]{1,2,0:T(8,128)} %bitcast.26), calls=%async_computation.5 | async-start | bytes 2097152 | tf_op jit(solution)/shard_map/all_to_all | solution.py:43
  150.2 84.5 %all-gather.9.cloned.1.call-start = ((), (), s32[]{:S(2)}) async-start(), calls=%async_computation.8 | async-start | bytes 4456448 | tf_op jit(solution)/shard_map/all_gather | solution.py:51
  157.3 18.7 %copy-start.2 = (f32[16384]{0:T(1024)S(1)}, f32[16384]{0:T(1024)}, u32[]{:S(2)}) copy-start(f32[16384]{0:T(1024)} %reshape.83) | copy-start | bytes 196612
  157.3 20.2 %copy-start.9 = (s32[256]{0:T(256)S(1)}, s32[256]{0:T(256)}, u32[]{:S(2)}) copy-start(s32[256]{0:T(256)} %param.13) | copy-start | bytes 3076
  176.8 159.0 %all-gather.7.cloned.1.call-start = ((), (), s32[]{:S(2)}) async-start(), calls=%async_computation.7 | async-start | bytes 8912896 | tf_op jit(solution)/shard_map/all_gather | solution.py:115
Sparse Core Ops, SparseCore 0:
  22.6 55.5 all-gather.4
  176.9 57.8 all-gather.8
  236.5 99.1 all-gather.6
